TPU v7x, 128 devices: a whole 4x4x4 slice. The times are simulated.
128 devices in a mesh: wide: 16 (over y_lo, z, core), narrow: 8 (over x, y_hi).
Axes of the slice: x: 4, y: 4 (y_hi: 2, y_lo: 2; y = y_hi * 2 + y_lo), z: 4, core: 2. Of those that a mesh axis runs over, the one named last changes fastest.
Arguments:
- fields: float32 [5, 16, 64, 256], P(None, 'wide', 'narrow'), may hold values from -2.1 to 6.1, as said below
- prior_modes: bfloat16 [124, 5, 16, 16384], P(None, None, 'wide', 'narrow'), may hold values from -360 to 360, as said below
Outputs:
- flow_state: float32 [5, 16, 64, 256], P(None, 'wide', 'narrow')
- factor: float32 [128, 128], replicated
Inputs may be any that keep to these rules, and one draw needn't show every extreme that they name: `fields`: density and pressure lie in 0.6 to 1.4, each velocity component below 1.5 in magnitude. `prior_modes`: the columns are linearly independent.
All inputs are finite; a program needn't handle non-finite values.
Results may differ from a plain program's by a relative error of at most 0.0014.
Values may be sent and summed in bfloat16 or wider, within the bound.
No kernel may reach another device: no remote copies, remote signals or barrier semaphores. Data moves between devices by JAX's collectives and lax.ppermute only.
A program may use at most 64 MiB of HBM per device.

v0:
```python
import jax
import jax.numpy as jnp
from jax import lax
from jax.sharding import PartitionSpec as P

STEPS = 2
GAMMA = 1.4
TIME_STEP = 0.25
VISCOSITY = 0.15


def extended(block, sides, width):
    for axis, dim in sides:
        count = lax.axis_size(axis)
        forward = [(i, i + 1) for i in range(count - 1)]
        forward.append((count - 1, 0))
        backward = [(target, source) for source, target in forward]
        low = lax.ppermute(
            lax.slice_in_dim(block, block.shape[dim] - width, None, axis=dim), axis, forward
        )
        high = lax.ppermute(lax.slice_in_dim(block, 0, width, axis=dim), axis, backward)
        block = jnp.concatenate([low, block, high], axis=dim)
    return block


def flux_of(current, dim_index):
    density = current[0]
    momentum = current[1:4]
    energy = current[4]
    vel_d = momentum[dim_index] / density
    pressure = (GAMMA - 1.0) * (
        energy
        - 0.5
        * (momentum[0] * momentum[0] + momentum[1] * momentum[1] + momentum[2] * momentum[2])
        / density
    )
    components = [
        momentum[dim_index],
        momentum[0] * vel_d,
        momentum[1] * vel_d,
        momentum[2] * vel_d,
        (energy + pressure) * vel_d,
    ]
    components[1 + dim_index] = components[1 + dim_index] + pressure
    return jnp.stack(components)


def tendency(current):
    padded = extended(current.astype(jnp.bfloat16), (("wide", 1), ("narrow", 2)), 1).astype(
        current.dtype
    )
    flux_x = flux_of(padded[:, :, 1:-1], 0)
    flux_y = flux_of(padded[:, 1:-1, :], 1)
    flux_z = flux_of(current, 2)
    divergence = (
        flux_x[:, 2:]
        - flux_x[:, :-2]
        + (flux_y[:, :, 2:] - flux_y[:, :, :-2])
        + (jnp.roll(flux_z, -1, 3) - jnp.roll(flux_z, 1, 3))
    )
    laplace = (
        padded[:, 2:, 1:-1]
        + padded[:, :-2, 1:-1]
        + padded[:, 1:-1, 2:]
        + padded[:, 1:-1, :-2]
        + jnp.roll(current, -1, 3)
        + jnp.roll(current, 1, 3)
        - 6.0 * current
    )
    return -0.5 * divergence + VISCOSITY * laplace


def local(fields, prior_modes):
    wide_count = lax.axis_size("wide")
    narrow_count = lax.axis_size("narrow")
    cells_x, cells_y, cells_z = (fields.shape[1], fields.shape[2], fields.shape[3])
    inverse_cells = 1.0 / (cells_x * wide_count * cells_y * narrow_count * cells_z)
    flat_modes = prior_modes.reshape(prior_modes.shape[0], -1)
    contract = (((1,), (1,)), ((), ()))
    gram_modes = lax.dot_general(
        flat_modes, flat_modes, contract, preferred_element_type=jnp.float32
    )
    current = fields
    snapshots = []
    for step_index in range(STEPS):
        section_one = current + TIME_STEP * tendency(current)
        snapshots.append(section_one.astype(jnp.bfloat16))
        current = 0.5 * current + 0.5 * (section_one + TIME_STEP * tendency(section_one))
        snapshots.append(current.astype(jnp.bfloat16))
    arrived = lax.all_to_all(
        jnp.stack(snapshots), "narrow", split_axis=4, concat_axis=3, tiled=True
    )
    snap_rows = jnp.swapaxes(arrived, 3, 4).reshape(arrived.shape[0], -1)
    cross_gram = lax.dot_general(
        flat_modes, snap_rows, contract, preferred_element_type=jnp.float32
    )
    snap_gram = lax.dot_general(snap_rows, snap_rows, contract, preferred_element_type=jnp.float32)
    gram_local = jnp.concatenate(
        [
            jnp.concatenate([gram_modes, cross_gram], 1),
            jnp.concatenate([cross_gram.T, snap_gram], 1),
        ],
        0,
    )
    gram_local = gram_local * inverse_cells
    devices = wide_count * narrow_count
    everywhere = ("wide", "narrow")
    pieces = gram_local.reshape(devices, 1, -1)
    pieces = lax.all_to_all(pieces, everywhere, split_axis=0, concat_axis=0, tiled=True)
    piece = jnp.sum(pieces, axis=0, keepdims=True)
    copies = jnp.broadcast_to(piece, pieces.shape)
    copies = lax.all_to_all(copies, everywhere, split_axis=0, concat_axis=0, tiled=True)
    gram_whole = copies.reshape(gram_local.shape)
    factor = jnp.linalg.cholesky(gram_whole).T
    return (current, factor)


def solution(mesh):
    placed = (P(None, "wide", "narrow", None), P(None, None, "wide", "narrow"))
    return jax.shard_map(
        local,
        mesh=mesh,
        in_specs=placed,
        out_specs=(P(None, "wide", "narrow", None), P()),
        check_vma=False,
    )
```

profile of v0, /device:TPU:1, one launch (start us, length us, event | category | flops | bytes accessed | tf_op | source)
XLA Modules:
  0.0 132.0 jit_solution(1061865496528465805)
XLA Ops:
  0.6 0.8 convert_element_type.30
  1.4 1.4 %collective-permute-start.1 = (bf16[5,1,8,256]{3,2,1,0:T(8,128)(2,1)S(1)}, bf16[5,1,8,256]{3,2,1,0:T(8,128)(2,1)S(1)}, u32[]{:S(2)}, u32[]{:S(2)}) collective-permute-start(bf16[5,1,8,256]{3,2,1,0:T(8,128)(2,1)S(1)} %convert_element_type.30), channel_id=1, source_target_pairs={{8,0},{16,8},{24,16},{32,24},{40,32},{48,40},{56,48},{64,56},{72,6... | collective-permute-start | bytes 61448 | tf_op jit(solution)/shard_map/ppermute | solution.py:21
  2.8 1.6 %collective-permute-start = (bf16[5,1,8,256]{3,2,1,0:T(8,128)(2,1)S(1)}, bf16[5,1,8,256]{3,2,1,0:T(8,128)(2,1)S(1)}, u32[]{:S(2)}, u32[]{:S(2)}) collective-permute-start(bf16[5,1,8,256]{3,2,1,0:T(8,128)(2,1)S(1)} %convert_element_type.30), channel_id=1, source_target_pairs={{0,8},{8,16},{16,24},{24,32},{32,40},{40,48},{48,56},{56,64},{64,7... | collective-permute-start | bytes 61448 | tf_op jit(solution)/shard_map/ppermute | solution.py:18
  5.1 0.8 constant_dynamic-update-slice_fusion.13
  6.6 0.8 constant_dynamic-update-slice_fusion.11
  8.1 0.9 fusion.98
  9.1 5.2 %collective-permute-start.3 = (bf16[5,3,1,256]{3,1,2,0:T(4,128)(2,1)S(1)}, bf16[5,3,1,256]{3,1,2,0:T(4,128)(2,1)S(1)}, u32[]{:S(2)}, u32[]{:S(2)}) collective-permute-start(bf16[5,3,1,256]{3,1,2,0:T(4,128)(2,1)S(1)} %copy.436), channel_id=1, source_target_pairs={{1,0},{2,1},{3,2},{4,3},{5,4},{6,5},{7,6},{0,7},{9,8},{10,9},{11,1... | collective-permute-start | bytes 23048 | tf_op jit(solution)/shard_map/ppermute | solution.py:21
  14.3 0.8 fusion.99
  15.2 5.3 %collective-permute-done.2 = bf16[5,3,1,256]{3,1,2,0:T(4,128)(2,1)S(1)} collective-permute-done((bf16[5,3,1,256]{3,1,2,0:T(4,128)(2,1)S(1)}, bf16[5,3,1,256]{3,1,2,0:T(4,128)(2,1)S(1)}, u32[]{:S(2)}, u32[]{:S(2)}) %collective-permute-start.2) | collective-permute-done | bytes 7712 | tf_op jit(solution)/shard_map/ppermute | solution.py:18
  20.8 0.9 fusion.83
  21.6 4.9 %collective-permute-start.5 = (bf16[5,1,8,256]{3,2,0,1:T(8,128)(2,1)S(1)}, bf16[5,1,8,256]{3,2,0,1:T(8,128)(2,1)S(1)}, u32[]{:S(2)}, u32[]{:S(2)}) collective-permute-start(bf16[5,1,8,256]{3,2,0,1:T(8,128)(2,1)S(1)} %get-tuple-element.65), channel_id=1, source_target_pairs={{8,0},{16,8},{24,16},{32,24},{40,32},{48,40},{56,48},{64,56},{72,6... | collective-permute-start | bytes 61448 | tf_op jit(solution)/shard_map/ppermute | solution.py:21
  27.4 1.0 collective-permute-done.4
  29.1 2.3 %collective-permute-start.6 = (bf16[5,3,1,256]{3,1,2,0:T(4,128)(2,1)S(1)}, bf16[5,3,1,256]{3,1,2,0:T(4,128)(2,1)S(1)}, u32[]{:S(2)}, u32[]{:S(2)}) collective-permute-start(bf16[5,3,1,256]{3,1,2,0:T(4,128)(2,1)S(1)} %copy.388), channel_id=1, source_target_pairs={{0,1},{1,2},{2,3},{3,4},{4,5},{5,6},{6,7},{7,0},{8,9},{9,10},{10,1... | collective-permute-start | bytes 23048 | tf_op jit(solution)/shard_map/ppermute | solution.py:18
  31.5 1.1 collective-permute-done.7
  32.6 2.6 %collective-permute-done.6 = bf16[5,3,1,256]{3,1,2,0:T(4,128)(2,1)S(1)} collective-permute-done((bf16[5,3,1,256]{3,1,2,0:T(4,128)(2,1)S(1)}, bf16[5,3,1,256]{3,1,2,0:T(4,128)(2,1)S(1)}, u32[]{:S(2)}, u32[]{:S(2)}) %collective-permute-start.6) | collective-permute-done | bytes 7712 | tf_op jit(solution)/shard_map/ppermute | solution.py:18
  35.8 6.1 %collective-permute-start.9 = (bf16[5,1,8,256]{3,2,0,1:T(8,128)(2,1)S(1)}, bf16[5,1,8,256]{3,2,0,1:T(8,128)(2,1)S(1)}, u32[]{:S(2)}, u32[]{:S(2)}) collective-permute-start(bf16[5,1,8,256]{3,2,0,1:T(8,128)(2,1)S(1)} %fusion.78), channel_id=1, source_target_pairs={{8,0},{16,8},{24,16},{32,24},{40,32},{48,40},{56,48},{64,56},{72,6... | collective-permute-start | bytes 61448 | tf_op jit(solution)/shard_map/ppermute | solution.py:21
  43.3 2.9 %collective-permute-start.10 = (bf16[5,3,1,256]{3,1,2,0:T(4,128)(2,1)S(1)}, bf16[5,3,1,256]{3,1,2,0:T(4,128)(2,1)S(1)}, u32[]{:S(2)}, u32[]{:S(2)}) collective-permute-start(bf16[5,3,1,256]{3,1,2,0:T(4,128)(2,1)S(1)} %copy.400), channel_id=1, source_target_pairs={{0,1},{1,2},{2,3},{3,4},{4,5},{5,6},{6,7},{7,0},{8,9},{9,10},{10,1... | collective-permute-start | bytes 23048 | tf_op jit(solution)/shard_map/ppermute | solution.py:18
  46.2 1.0 collective-permute-done.11
  47.3 2.2 %collective-permute-done.10 = bf16[5,3,1,256]{3,1,2,0:T(4,128)(2,1)S(1)} collective-permute-done((bf16[5,3,1,256]{3,1,2,0:T(4,128)(2,1)S(1)}, bf16[5,3,1,256]{3,1,2,0:T(4,128)(2,1)S(1)}, u32[]{:S(2)}, u32[]{:S(2)}) %collective-permute-start.10) | collective-permute-done | bytes 7712 | tf_op jit(solution)/shard_map/ppermute | solution.py:18
  49.9 5.4 %collective-permute-start.13 = (bf16[5,1,8,256]{3,2,0,1:T(8,128)(2,1)S(1)}, bf16[5,1,8,256]{3,2,0,1:T(8,128)(2,1)S(1)}, u32[]{:S(2)}, u32[]{:S(2)}) collective-permute-start(bf16[5,1,8,256]{3,2,0,1:T(8,128)(2,1)S(1)} %get-tuple-element.31), channel_id=1, source_target_pairs={{8,0},{16,8},{24,16},{32,24},{40,32},{48,40},{56,48},{64,56},{72,6... | collective-permute-start | bytes 61448 | tf_op jit(solution)/shard_map/ppermute | solution.py:21
  56.7 2.9 %collective-permute-start.14 = (bf16[5,3,1,256]{3,1,2,0:T(4,128)(2,1)S(1)}, bf16[5,3,1,256]{3,1,2,0:T(4,128)(2,1)S(1)}, u32[]{:S(2)}, u32[]{:S(2)}) collective-permute-start(bf16[5,3,1,256]{3,1,2,0:T(4,128)(2,1)S(1)} %copy.411), channel_id=1, source_target_pairs={{0,1},{1,2},{2,3},{3,4},{4,5},{5,6},{6,7},{7,0},{8,9},{9,10},{10,1... | collective-permute-start | bytes 23048 | tf_op jit(solution)/shard_map/ppermute | solution.py:18
  59.7 1.0 collective-permute-done.15
  60.7 2.2 %collective-permute-done.14 = bf16[5,3,1,256]{3,1,2,0:T(4,128)(2,1)S(1)} collective-permute-done((bf16[5,3,1,256]{3,1,2,0:T(4,128)(2,1)S(1)}, bf16[5,3,1,256]{3,1,2,0:T(4,128)(2,1)S(1)}, u32[]{:S(2)}, u32[]{:S(2)}) %collective-permute-start.14) | collective-permute-done | bytes 7712 | tf_op jit(solution)/shard_map/ppermute | solution.py:18
  64.7 2.0 %reshape.669 = bf16[8,2,2560]{2,1,0:T(2,128)(2,1)} reshape(bf16[256,5,1,4,8]{4,3,2,1,0:T(4,128)(2,1)S(1)} %bitcast.162) | data formatting | bytes 163840
  66.7 3.5 %all-to-all-start = ((bf16[8,2,2560]{2,1,0:T(2,128)(2,1)}), bf16[8,2,2560]{2,1,0:T(2,128)(2,1)S(1)}, u32[]{:S(2)}, u32[]{:S(2)}) async-start(bf16[8,2,2560]{2,1,0:T(2,128)(2,1)} %reshape.669), calls=%async_computation | async-start | bytes 163840 | tf_op jit(solution)/shard_map/all_to_all | solution.py:90
  70.2 3.4 %fusion.2 = f32[124,124]{0,1:T(8,128)S(1)} fusion(bf16[124,5,1,2048]{3,0,2,1:T(8,128)(2,1)} %param.3), kind=kOutput, calls=%fused_computation.2 | convolution fusion | flops 314900480 | bytes 2601024 | tf_op jit(solution)/shard_map/dot_general | solution.py:80
  73.6 3.3 %copy.426 = bf16[124,5,1,2048]{0,3,1,2:T(8,128)(2,1)S(1)} copy(bf16[124,5,1,2048]{3,0,2,1:T(8,128)(2,1)} %param.3) | data formatting | bytes 5079040 | tf_op args[1]
  76.9 2.6 %reshape.670 = bf16[256,5,1,4,8]{4,3,2,1,0:T(4,128)(2,1)} reshape(bf16[8,2,2560]{2,1,0:T(2,128)(2,1)S(1)} %all-to-all-done) | data formatting | bytes 163840
  79.5 1.8 %copy.423 = bf16[4,5,1,8,8,32]{5,3,4,1,0,2:T(8,128)(2,1)S(1)} copy(bf16[4,5,1,8,8,32]{3,0,1,5,4,2:T(4,128)(2,1)} %bitcast.163) | data formatting | bytes 163840 | tf_op jit(solution)/shard_map/all_to_all | solution.py:90
  82.9 21.2 %all_to_all.28 = f32[128,1,128]{2,1,0:T(1,128)S(1)} all-to-all(f32[128,1,128]{2,1,0:T(1,128)S(1)} %copy.428), channel_id=1, replica_groups=mesh['wide'=16,'narrow'=8] {'wide','narrow'}, dimensions={0} | all-to-all | bytes 131072 | tf_op jit(solution)/shard_map/all_to_all | solution.py:109
  104.3 13.8 %all_to_all.29 = f32[128,1,128]{2,1,0:T(1,128)S(1)} all-to-all(f32[128,1,128]{2,1,0:T(1,128)S(1)} %broadcast_in_dim.3), channel_id=1, replica_groups=mesh['wide'=16,'narrow'=8] {'wide','narrow'}, dimensions={0} | all-to-all | bytes 131072 | tf_op jit(solution)/shard_map/all_to_all | solution.py:112
  118.2 11.7 %cholesky.18 = f32[128,128]{1,0:T(8,128)S(1)} custom-call(f32[128,128]{1,0:T(8,128)S(1)} %fusion.6), custom_call_target="Cholesky" | custom-call | tf_op jit(solution)/shard_map/jit(cholesky)/cholesky | solution.py:114
  (138 shorter events, 13.1 us)
Async XLA Ops:
  1.4 7.6 %collective-permute-start.1 = (bf16[5,1,8,256]{3,2,1,0:T(8,128)(2,1)S(1)}, bf16[5,1,8,256]{3,2,1,0:T(8,128)(2,1)S(1)}, u32[]{:S(2)}, u32[]{:S(2)}) collective-permute-start(bf16[5,1,8,256]{3,2,1,0:T(8,128)(2,1)S(1)} %convert_element_type.30), channel_id=1, source_target_pairs={{8,0},{16,8},{24,16},{32,24},{40,32},{48,40},{56,48},{64,56},{72,6... | collective-permute-start | bytes 61448 | tf_op jit(solution)/shard_map/ppermute | solution.py:21
  2.8 6.3 %collective-permute-start = (bf16[5,1,8,256]{3,2,1,0:T(8,128)(2,1)S(1)}, bf16[5,1,8,256]{3,2,1,0:T(8,128)(2,1)S(1)}, u32[]{:S(2)}, u32[]{:S(2)}) collective-permute-start(bf16[5,1,8,256]{3,2,1,0:T(8,128)(2,1)S(1)} %convert_element_type.30), channel_id=1, source_target_pairs={{0,8},{8,16},{16,24},{24,32},{32,40},{40,48},{48,56},{56,64},{64,7... | collective-permute-start | bytes 61448 | tf_op jit(solution)/shard_map/ppermute | solution.py:18
  5.1 30.4 %copy-start = (f32[5,1,8,256]{3,2,1,0:T(8,128)S(1)}, f32[5,1,8,256]{3,2,1,0:T(8,128)}, u32[]{:S(2)}) copy-start(f32[5,1,8,256]{3,2,1,0:T(8,128)} %param.2) | copy-start | bytes 122884
  9.1 6.0 %collective-permute-start.3 = (bf16[5,3,1,256]{3,1,2,0:T(4,128)(2,1)S(1)}, bf16[5,3,1,256]{3,1,2,0:T(4,128)(2,1)S(1)}, u32[]{:S(2)}, u32[]{:S(2)}) collective-permute-start(bf16[5,3,1,256]{3,1,2,0:T(4,128)(2,1)S(1)} %copy.436), channel_id=1, source_target_pairs={{1,0},{2,1},{3,2},{4,3},{5,4},{6,5},{7,6},{0,7},{9,8},{10,9},{11,1... | collective-permute-start | bytes 23048 | tf_op jit(solution)/shard_map/ppermute | solution.py:21
  14.3 6.1 %collective-permute-start.2 = (bf16[5,3,1,256]{3,1,2,0:T(4,128)(2,1)S(1)}, bf16[5,3,1,256]{3,1,2,0:T(4,128)(2,1)S(1)}, u32[]{:S(2)}, u32[]{:S(2)}) collective-permute-start(bf16[5,3,1,256]{3,1,2,0:T(4,128)(2,1)S(1)} %copy.435), channel_id=1, source_target_pairs={{0,1},{1,2},{2,3},{3,4},{4,5},{5,6},{6,7},{7,0},{8,9},{9,10},{10,1... | collective-permute-start | bytes 23048 | tf_op jit(solution)/shard_map/ppermute | solution.py:18
  21.6 5.7 %collective-permute-start.5 = (bf16[5,1,8,256]{3,2,0,1:T(8,128)(2,1)S(1)}, bf16[5,1,8,256]{3,2,0,1:T(8,128)(2,1)S(1)}, u32[]{:S(2)}, u32[]{:S(2)}) collective-permute-start(bf16[5,1,8,256]{3,2,0,1:T(8,128)(2,1)S(1)} %get-tuple-element.65), channel_id=1, source_target_pairs={{8,0},{16,8},{24,16},{32,24},{40,32},{48,40},{56,48},{64,56},{72,6... | collective-permute-start | bytes 61448 | tf_op jit(solution)/shard_map/ppermute | solution.py:21
  26.5 1.8 %collective-permute-start.4 = (bf16[5,1,8,256]{3,2,0,1:T(8,128)(2,1)S(1)}, bf16[5,1,8,256]{3,2,0,1:T(8,128)(2,1)S(1)}, u32[]{:S(2)}, u32[]{:S(2)}) collective-permute-start(bf16[5,1,8,256]{3,2,0,1:T(8,128)(2,1)S(1)} %get-tuple-element.65), channel_id=1, source_target_pairs={{0,8},{8,16},{16,24},{24,32},{32,40},{40,48},{48,56},{56,64},{64,7... | collective-permute-start | bytes 61448 | tf_op jit(solution)/shard_map/ppermute | solution.py:18
  28.4 4.2 %collective-permute-start.7 = (bf16[5,3,1,256]{3,1,2,0:T(4,128)(2,1)S(1)}, bf16[5,3,1,256]{3,1,2,0:T(4,128)(2,1)S(1)}, u32[]{:S(2)}, u32[]{:S(2)}) collective-permute-start(bf16[5,3,1,256]{3,1,2,0:T(4,128)(2,1)S(1)} %copy.389), channel_id=1, source_target_pairs={{1,0},{2,1},{3,2},{4,3},{5,4},{6,5},{7,6},{0,7},{9,8},{10,9},{11,1... | collective-permute-start | bytes 23048 | tf_op jit(solution)/shard_map/ppermute | solution.py:21
  29.1 6.1 %collective-permute-start.6 = (bf16[5,3,1,256]{3,1,2,0:T(4,128)(2,1)S(1)}, bf16[5,3,1,256]{3,1,2,0:T(4,128)(2,1)S(1)}, u32[]{:S(2)}, u32[]{:S(2)}) collective-permute-start(bf16[5,3,1,256]{3,1,2,0:T(4,128)(2,1)S(1)} %copy.388), channel_id=1, source_target_pairs={{0,1},{1,2},{2,3},{3,4},{4,5},{5,6},{6,7},{7,0},{8,9},{9,10},{10,1... | collective-permute-start | bytes 23048 | tf_op jit(solution)/shard_map/ppermute | solution.py:18
  35.8 7.0 %collective-permute-start.9 = (bf16[5,1,8,256]{3,2,0,1:T(8,128)(2,1)S(1)}, bf16[5,1,8,256]{3,2,0,1:T(8,128)(2,1)S(1)}, u32[]{:S(2)}, u32[]{:S(2)}) collective-permute-start(bf16[5,1,8,256]{3,2,0,1:T(8,128)(2,1)S(1)} %fusion.78), channel_id=1, source_target_pairs={{8,0},{16,8},{24,16},{32,24},{40,32},{48,40},{56,48},{64,56},{72,6... | collective-permute-start | bytes 61448 | tf_op jit(solution)/shard_map/ppermute | solution.py:21
  41.9 1.2 collective-permute-start.8
  43.2 4.1 %collective-permute-start.11 = (bf16[5,3,1,256]{3,1,2,0:T(4,128)(2,1)S(1)}, bf16[5,3,1,256]{3,1,2,0:T(4,128)(2,1)S(1)}, u32[]{:S(2)}, u32[]{:S(2)}) collective-permute-start(bf16[5,3,1,256]{3,1,2,0:T(4,128)(2,1)S(1)} %copy.401), channel_id=1, source_target_pairs={{1,0},{2,1},{3,2},{4,3},{5,4},{6,5},{7,6},{0,7},{9,8},{10,9},{11,1... | collective-permute-start | bytes 23048 | tf_op jit(solution)/shard_map/ppermute | solution.py:21
  43.3 6.2 %collective-permute-start.10 = (bf16[5,3,1,256]{3,1,2,0:T(4,128)(2,1)S(1)}, bf16[5,3,1,256]{3,1,2,0:T(4,128)(2,1)S(1)}, u32[]{:S(2)}, u32[]{:S(2)}) collective-permute-start(bf16[5,3,1,256]{3,1,2,0:T(4,128)(2,1)S(1)} %copy.400), channel_id=1, source_target_pairs={{0,1},{1,2},{2,3},{3,4},{4,5},{5,6},{6,7},{7,0},{8,9},{9,10},{10,1... | collective-permute-start | bytes 23048 | tf_op jit(solution)/shard_map/ppermute | solution.py:18
  49.9 6.3 %collective-permute-start.13 = (bf16[5,1,8,256]{3,2,0,1:T(8,128)(2,1)S(1)}, bf16[5,1,8,256]{3,2,0,1:T(8,128)(2,1)S(1)}, u32[]{:S(2)}, u32[]{:S(2)}) collective-permute-start(bf16[5,1,8,256]{3,2,0,1:T(8,128)(2,1)S(1)} %get-tuple-element.31), channel_id=1, source_target_pairs={{8,0},{16,8},{24,16},{32,24},{40,32},{48,40},{56,48},{64,56},{72,6... | collective-permute-start | bytes 61448 | tf_op jit(solution)/shard_map/ppermute | solution.py:21
  55.3 1.2 collective-permute-start.12
  56.6 4.1 %collective-permute-start.15 = (bf16[5,3,1,256]{3,1,2,0:T(4,128)(2,1)S(1)}, bf16[5,3,1,256]{3,1,2,0:T(4,128)(2,1)S(1)}, u32[]{:S(2)}, u32[]{:S(2)}) collective-permute-start(bf16[5,3,1,256]{3,1,2,0:T(4,128)(2,1)S(1)} %copy.412), channel_id=1, source_target_pairs={{1,0},{2,1},{3,2},{4,3},{5,4},{6,5},{7,6},{0,7},{9,8},{10,9},{11,1... | collective-permute-start | bytes 23048 | tf_op jit(solution)/shard_map/ppermute | solution.py:21
  56.7 6.2 %collective-permute-start.14 = (bf16[5,3,1,256]{3,1,2,0:T(4,128)(2,1)S(1)}, bf16[5,3,1,256]{3,1,2,0:T(4,128)(2,1)S(1)}, u32[]{:S(2)}, u32[]{:S(2)}) collective-permute-start(bf16[5,3,1,256]{3,1,2,0:T(4,128)(2,1)S(1)} %copy.411), channel_id=1, source_target_pairs={{0,1},{1,2},{2,3},{3,4},{4,5},{5,6},{6,7},{7,0},{8,9},{9,10},{10,1... | collective-permute-start | bytes 23048 | tf_op jit(solution)/shard_map/ppermute | solution.py:18
  66.7 10.2 %all-to-all-start = ((bf16[8,2,2560]{2,1,0:T(2,128)(2,1)}), bf16[8,2,2560]{2,1,0:T(2,128)(2,1)S(1)}, u32[]{:S(2)}, u32[]{:S(2)}) async-start(bf16[8,2,2560]{2,1,0:T(2,128)(2,1)} %reshape.669), calls=%async_computation | async-start | bytes 163840 | tf_op jit(solution)/shard_map/all_to_all | solution.py:90
where the time goes:
time: 133 us; the launch traced here: 132 us
  starting transfers between devices  37.2 us (28%)
  blocking collectives  35 us (26%)
  other arithmetic  20.1 us (15%)
  waiting for transfers between devices  18.8 us (14%)
  local copies, waits for them, and re-layouts  15.5 us (12%)
  matrix products  4.09 us (3%)
    ppermute x8, starting transfers between devices, extended(): lax.ppermute(lax.slice_in_dim(block, 0, width, axis=dim), axis, backward)  23.8 us
    all_to_all x1, blocking collectives, local(): lax.all_to_all(pieces, everywhere, split_axis=0, concat_axis=0, tiled=True)  21.2 us
    ppermute x8, waiting for transfers between devices, extended(): lax.ppermute(lax.slice_in_dim(block, block.shape[dim] - width, None, axis...  13.9 us
    all_to_all x1, blocking collectives, local(): lax.all_to_all(copies, everywhere, split_axis=0, concat_axis=0, tiled=True)  13.8 us
    another operation x3, other arithmetic, local(): factor = jnp.linalg.cholesky(gram_whole).T  12.4 us
    ppermute x8, starting transfers between devices, extended(): lax.ppermute(lax.slice_in_dim(block, block.shape[dim] - width, None, axis...  9.89 us
    unnamed x16, local copies, waits for them, and re-layouts  9.42 us
    ppermute x8, waiting for transfers between devices, extended(): lax.ppermute(lax.slice_in_dim(block, 0, width, axis=dim), axis, backward)  4.85 us
  transfers between devices with their start and end apart: 17, of which 13 were waited for; matrix products, arithmetic and copies ran while one was open for 10% of the time, Pallas kernels for 0%

commit v1 on v0

--- a/solution.py
+++ b/solution.py
@@ -87,8 +87,14 @@
         snapshots.append(section_one.astype(jnp.bfloat16))
         current = 0.5 * current + 0.5 * (section_one + TIME_STEP * tendency(section_one))
         snapshots.append(current.astype(jnp.bfloat16))
-    arrived = lax.all_to_all(
-        jnp.stack(snapshots), "narrow", split_axis=4, concat_axis=3, tiled=True
+    arrived = jnp.concatenate(
+        lax.all_to_all(
+            jnp.stack(jnp.split(jnp.stack(snapshots), lax.axis_size("narrow"), axis=4)),
+            "narrow",
+            0,
+            0,
+        ),
+        axis=3,
     )
     snap_rows = jnp.swapaxes(arrived, 3, 4).reshape(arrived.shape[0], -1)
     cross_gram = lax.dot_general(

time: 133 us -> 125 us (0.940)
  local copies, waits for them, and re-layouts: 15.5 us -> 9.92 us
  waiting for transfers between devices: 18.8 us -> 21.4 us
  matrix products: 4.09 us -> 1.55 us
  blocking collectives: 35 us -> 32.8 us
    unnamed x16 -> x23, local copies, waits for them, and re-layouts: 9.42 us -> 6.39 us
    dot_general x1, matrix products: 3.37 us -> 0.84 us  [local(): lax.dot_general(flat_modes, flat_modes, contract, preferred_element_type=...]
    all_to_all x1, waiting for transfers between devices: 0.01 us -> 2.4 us  [local(): lax.all_to_all(jnp.stack(jnp.split(jnp.stack(snapshots), lax.axis_size('n...]
    all_to_all x1, blocking collectives: 21.2 us -> 19.1 us  [local(): lax.all_to_all(pieces, everywhere, split_axis=0, concat_axis=0, tiled=True)]
    all_to_all x2 -> x0, local copies, waits for them, and re-layouts: 2 us -> none  [local(): lax.all_to_all(jnp.stack(snapshots), 'narrow', split_axis=4, concat_axis=...]
  transfers between devices with their start and end apart: 17 -> 17, of which waited for: 13 -> 14; matrix products, arithmetic and copies ran while one was open for 10% -> 8% of each run, Pallas kernels for 0% -> 0%
where the time goes in v1:
time: 125 us; the launch traced here: 124 us
  starting transfers between devices  37.1 us (30%)
  blocking collectives  32.8 us (26%)
  waiting for transfers between devices  21.4 us (17%)
  other arithmetic  20.1 us (16%)
  local copies, waits for them, and re-layouts  9.92 us (8%)
  matrix products  1.55 us (1%)
  between operations  1.25 us (1%)
    ppermute x8, starting transfers between devices, extended(): lax.ppermute(lax.slice_in_dim(block, 0, width, axis=dim), axis, backward)  23.8 us
    all_to_all x1, blocking collectives, local(): lax.all_to_all(pieces, everywhere, split_axis=0, concat_axis=0, tiled=True)  19.1 us
    ppermute x8, waiting for transfers between devices, extended(): lax.ppermute(lax.slice_in_dim(block, block.shape[dim] - width, None, axis...  14 us
    all_to_all x1, blocking collectives, local(): lax.all_to_all(copies, everywhere, split_axis=0, concat_axis=0, tiled=True)  13.8 us
    another operation x3, other arithmetic, local(): factor = jnp.linalg.cholesky(gram_whole).T  12.4 us
    ppermute x8, starting transfers between devices, extended(): lax.ppermute(lax.slice_in_dim(block, block.shape[dim] - width, None, axis...  9.92 us
    unnamed x23, local copies, waits for them, and re-layouts  6.39 us
    ppermute x8, waiting for transfers between devices, extended(): lax.ppermute(lax.slice_in_dim(block, 0, width, axis=dim), axis, backward)  5.03 us
  transfers between devices with their start and end apart: 17, of which 14 were waited for; matrix products, arithmetic and copies ran while one was open for 8% of the time, Pallas kernels for 0%

profile of v1, /device:TPU:1, one launch (start us, length us, event | category | flops | bytes accessed | tf_op | source)
XLA Modules:
  0.0 124.2 jit_solution(17621525473806025044)
XLA Ops:
  0.6 0.8 bitcast_convert_fusion
  1.5 1.4 %collective-permute-start.1 = (bf16[5,1,8,256]{3,2,0,1:T(8,128)(2,1)S(1)}, bf16[5,1,8,256]{3,2,0,1:T(8,128)(2,1)S(1)}, u32[]{:S(2)}, u32[]{:S(2)}) collective-permute-start(bf16[5,1,8,256]{3,2,0,1:T(8,128)(2,1)S(1)} %bitcast_convert_fusion), channel_id=1, source_target_pairs={{8,0},{16,8},{24,16},{32,24},{40,32},{48,40},{56,48},{64,56},{72,6... | collective-permute-start | bytes 61448 | tf_op jit(solution)/shard_map/ppermute | solution.py:21
  2.9 1.6 %collective-permute-start = (bf16[5,1,8,256]{3,2,0,1:T(8,128)(2,1)S(1)}, bf16[5,1,8,256]{3,2,0,1:T(8,128)(2,1)S(1)}, u32[]{:S(2)}, u32[]{:S(2)}) collective-permute-start(bf16[5,1,8,256]{3,2,0,1:T(8,128)(2,1)S(1)} %bitcast_convert_fusion), channel_id=1, source_target_pairs={{0,8},{8,16},{16,24},{24,32},{32,40},{40,48},{48,56},{56,64},{64,7... | collective-permute-start | bytes 61448 | tf_op jit(solution)/shard_map/ppermute | solution.py:18
  5.2 0.7 constant_dynamic-update-slice_fusion.13
  6.6 0.8 constant_dynamic-update-slice_fusion.11
  8.1 0.9 fusion.95
  9.1 5.2 %collective-permute-start.3 = (bf16[5,3,1,256]{3,2,0,1:T(2,128)(2,1)S(1)}, bf16[5,3,1,256]{3,2,0,1:T(2,128)(2,1)S(1)}, u32[]{:S(2)}, u32[]{:S(2)}) collective-permute-start(bf16[5,3,1,256]{3,2,0,1:T(2,128)(2,1)S(1)} %get-tuple-element.85), channel_id=1, source_target_pairs={{1,0},{2,1},{3,2},{4,3},{5,4},{6,5},{7,6},{0,7},{9,8},{10,9},{11,1... | collective-permute-start | bytes 23048 | tf_op jit(solution)/shard_map/ppermute | solution.py:21
  14.3 0.8 fusion.96
  15.2 5.3 %collective-permute-done.2 = bf16[5,3,1,256]{3,2,0,1:T(2,128)(2,1)S(1)} collective-permute-done((bf16[5,3,1,256]{3,2,0,1:T(2,128)(2,1)S(1)}, bf16[5,3,1,256]{3,2,0,1:T(2,128)(2,1)S(1)}, u32[]{:S(2)}, u32[]{:S(2)}) %collective-permute-start.2) | collective-permute-done | bytes 7712 | tf_op jit(solution)/shard_map/ppermute | solution.py:18
  20.8 0.9 fusion.81
  21.7 4.9 %collective-permute-start.5 = (bf16[5,1,8,256]{3,2,0,1:T(8,128)(2,1)S(1)}, bf16[5,1,8,256]{3,2,0,1:T(8,128)(2,1)S(1)}, u32[]{:S(2)}, u32[]{:S(2)}) collective-permute-start(bf16[5,1,8,256]{3,2,0,1:T(8,128)(2,1)S(1)} %get-tuple-element.59), channel_id=1, source_target_pairs={{8,0},{16,8},{24,16},{32,24},{40,32},{48,40},{56,48},{64,56},{72,6... | collective-permute-start | bytes 61448 | tf_op jit(solution)/shard_map/ppermute | solution.py:21
  27.4 0.9 collective-permute-done.4
  29.1 2.4 %collective-permute-start.6 = (bf16[5,3,1,256]{3,2,0,1:T(2,128)(2,1)S(1)}, bf16[5,3,1,256]{3,2,0,1:T(2,128)(2,1)S(1)}, u32[]{:S(2)}, u32[]{:S(2)}) collective-permute-start(bf16[5,3,1,256]{3,2,0,1:T(2,128)(2,1)S(1)} %get-tuple-element.82), channel_id=1, source_target_pairs={{0,1},{1,2},{2,3},{3,4},{4,5},{5,6},{6,7},{7,0},{8,9},{9,10},{10,1... | collective-permute-start | bytes 23048 | tf_op jit(solution)/shard_map/ppermute | solution.py:18
  31.5 1.1 collective-permute-done.7
  32.6 2.7 %collective-permute-done.6 = bf16[5,3,1,256]{3,2,0,1:T(2,128)(2,1)S(1)} collective-permute-done((bf16[5,3,1,256]{3,2,0,1:T(2,128)(2,1)S(1)}, bf16[5,3,1,256]{3,2,0,1:T(2,128)(2,1)S(1)}, u32[]{:S(2)}, u32[]{:S(2)}) %collective-permute-start.6) | collective-permute-done | bytes 7712 | tf_op jit(solution)/shard_map/ppermute | solution.py:18
  35.8 6.1 %collective-permute-start.9 = (bf16[5,1,8,256]{3,2,0,1:T(8,128)(2,1)S(1)}, bf16[5,1,8,256]{3,2,0,1:T(8,128)(2,1)S(1)}, u32[]{:S(2)}, u32[]{:S(2)}) collective-permute-start(bf16[5,1,8,256]{3,2,0,1:T(8,128)(2,1)S(1)} %fusion.75), channel_id=1, source_target_pairs={{8,0},{16,8},{24,16},{32,24},{40,32},{48,40},{56,48},{64,56},{72,6... | collective-permute-start | bytes 61448 | tf_op jit(solution)/shard_map/ppermute | solution.py:21
  43.2 3.0 %collective-permute-start.10 = (bf16[5,3,1,256]{3,2,0,1:T(2,128)(2,1)S(1)}, bf16[5,3,1,256]{3,2,0,1:T(2,128)(2,1)S(1)}, u32[]{:S(2)}, u32[]{:S(2)}) collective-permute-start(bf16[5,3,1,256]{3,2,0,1:T(2,128)(2,1)S(1)} %get-tuple-element.80), channel_id=1, source_target_pairs={{0,1},{1,2},{2,3},{3,4},{4,5},{5,6},{6,7},{7,0},{8,9},{9,10},{10,1... | collective-permute-start | bytes 23048 | tf_op jit(solution)/shard_map/ppermute | solution.py:18
  46.2 1.1 collective-permute-done.11
  47.3 2.2 %collective-permute-done.10 = bf16[5,3,1,256]{3,2,0,1:T(2,128)(2,1)S(1)} collective-permute-done((bf16[5,3,1,256]{3,2,0,1:T(2,128)(2,1)S(1)}, bf16[5,3,1,256]{3,2,0,1:T(2,128)(2,1)S(1)}, u32[]{:S(2)}, u32[]{:S(2)}) %collective-permute-start.10) | collective-permute-done | bytes 7712 | tf_op jit(solution)/shard_map/ppermute | solution.py:18
  49.9 5.4 %collective-permute-start.13 = (bf16[5,1,8,256]{3,2,0,1:T(8,128)(2,1)S(1)}, bf16[5,1,8,256]{3,2,0,1:T(8,128)(2,1)S(1)}, u32[]{:S(2)}, u32[]{:S(2)}) collective-permute-start(bf16[5,1,8,256]{3,2,0,1:T(8,128)(2,1)S(1)} %get-tuple-element.25), channel_id=1, source_target_pairs={{8,0},{16,8},{24,16},{32,24},{40,32},{48,40},{56,48},{64,56},{72,6... | collective-permute-start | bytes 61448 | tf_op jit(solution)/shard_map/ppermute | solution.py:21
  56.7 3.0 %collective-permute-start.14 = (bf16[5,3,1,256]{3,2,0,1:T(2,128)(2,1)S(1)}, bf16[5,3,1,256]{3,2,0,1:T(2,128)(2,1)S(1)}, u32[]{:S(2)}, u32[]{:S(2)}) collective-permute-start(bf16[5,3,1,256]{3,2,0,1:T(2,128)(2,1)S(1)} %get-tuple-element.78), channel_id=1, source_target_pairs={{0,1},{1,2},{2,3},{3,4},{4,5},{5,6},{6,7},{7,0},{8,9},{9,10},{10,1... | collective-permute-start | bytes 23048 | tf_op jit(solution)/shard_map/ppermute | solution.py:18
  59.7 1.0 collective-permute-done.15
  60.7 2.2 %collective-permute-done.14 = bf16[5,3,1,256]{3,2,0,1:T(2,128)(2,1)S(1)} collective-permute-done((bf16[5,3,1,256]{3,2,0,1:T(2,128)(2,1)S(1)}, bf16[5,3,1,256]{3,2,0,1:T(2,128)(2,1)S(1)}, u32[]{:S(2)}, u32[]{:S(2)}) %collective-permute-start.14) | collective-permute-done | bytes 7712 | tf_op jit(solution)/shard_map/ppermute | solution.py:18
  63.2 0.7 convert_bitcast_fusion
  64.6 0.9 reshape.677
  65.5 3.4 %all-to-all-start = ((bf16[8,2,2560]{2,1,0:T(2,128)(2,1)}), bf16[8,2,2560]{2,1,0:T(2,128)(2,1)S(1)}, u32[]{:S(2)}, u32[]{:S(2)}) async-start(bf16[8,2,2560]{2,1,0:T(2,128)(2,1)} %reshape.677), calls=%async_computation | async-start | bytes 163840 | tf_op jit(solution)/shard_map/all_to_all | solution.py:91
  68.9 0.8 fusion.2
  69.7 3.3 %copy.86 = bf16[124,5,1,2048]{0,3,1,2:T(8,128)(2,1)S(1)} copy(bf16[124,5,1,2048]{3,0,2,1:T(8,128)(2,1)} %param.3) | data formatting | bytes 5079040 | tf_op args[1]
  73.0 2.4 %all-to-all-done = bf16[8,2,2560]{2,1,0:T(2,128)(2,1)S(1)} async-done(((bf16[8,2,2560]{2,1,0:T(2,128)(2,1)}), bf16[8,2,2560]{2,1,0:T(2,128)(2,1)S(1)}, u32[]{:S(2)}, u32[]{:S(2)}) %all-to-all-start) | async-done | bytes 81952 | tf_op jit(solution)/shard_map/all_to_all | solution.py:91
  77.3 19.1 %all_to_all.15 = f32[128,1,128]{2,1,0:T(1,128)S(1)} all-to-all(f32[128,1,128]{2,1,0:T(1,128)S(1)} %copy.88), channel_id=1, replica_groups=mesh['wide'=16,'narrow'=8] {'wide','narrow'}, dimensions={0} | all-to-all | bytes 131072 | tf_op jit(solution)/shard_map/all_to_all | solution.py:115
  96.5 13.8 %all_to_all.16 = f32[128,1,128]{2,1,0:T(1,128)S(1)} all-to-all(f32[128,1,128]{2,1,0:T(1,128)S(1)} %broadcast_in_dim.3), channel_id=1, replica_groups=mesh['wide'=16,'narrow'=8] {'wide','narrow'}, dimensions={0} | all-to-all | bytes 131072 | tf_op jit(solution)/shard_map/all_to_all | solution.py:118
  110.4 11.7 %cholesky.18 = f32[128,128]{1,0:T(8,128)S(1)} custom-call(f32[128,128]{1,0:T(8,128)S(1)} %fusion.6), custom_call_target="Cholesky" | custom-call | tf_op jit(solution)/shard_map/jit(cholesky)/cholesky | solution.py:120
  (130 shorter events, 12.4 us)
Async XLA Ops:
  0.6 34.9 %copy-start = (f32[5,1,8,256]{3,2,1,0:T(8,128)S(1)}, f32[5,1,8,256]{3,2,1,0:T(8,128)}, u32[]{:S(2)}) copy-start(f32[5,1,8,256]{3,2,1,0:T(8,128)} %param.2) | copy-start | bytes 122884
  1.5 7.6 %collective-permute-start.1 = (bf16[5,1,8,256]{3,2,0,1:T(8,128)(2,1)S(1)}, bf16[5,1,8,256]{3,2,0,1:T(8,128)(2,1)S(1)}, u32[]{:S(2)}, u32[]{:S(2)}) collective-permute-start(bf16[5,1,8,256]{3,2,0,1:T(8,128)(2,1)S(1)} %bitcast_convert_fusion), channel_id=1, source_target_pairs={{8,0},{16,8},{24,16},{32,24},{40,32},{48,40},{56,48},{64,56},{72,6... | collective-permute-start | bytes 61448 | tf_op jit(solution)/shard_map/ppermute | solution.py:21
  2.9 6.2 %collective-permute-start = (bf16[5,1,8,256]{3,2,0,1:T(8,128)(2,1)S(1)}, bf16[5,1,8,256]{3,2,0,1:T(8,128)(2,1)S(1)}, u32[]{:S(2)}, u32[]{:S(2)}) collective-permute-start(bf16[5,1,8,256]{3,2,0,1:T(8,128)(2,1)S(1)} %bitcast_convert_fusion), channel_id=1, source_target_pairs={{0,8},{8,16},{16,24},{24,32},{32,40},{40,48},{48,56},{56,64},{64,7... | collective-permute-start | bytes 61448 | tf_op jit(solution)/shard_map/ppermute | solution.py:18
  9.1 6.0 %collective-permute-start.3 = (bf16[5,3,1,256]{3,2,0,1:T(2,128)(2,1)S(1)}, bf16[5,3,1,256]{3,2,0,1:T(2,128)(2,1)S(1)}, u32[]{:S(2)}, u32[]{:S(2)}) collective-permute-start(bf16[5,3,1,256]{3,2,0,1:T(2,128)(2,1)S(1)} %get-tuple-element.85), channel_id=1, source_target_pairs={{1,0},{2,1},{3,2},{4,3},{5,4},{6,5},{7,6},{0,7},{9,8},{10,9},{11,1... | collective-permute-start | bytes 23048 | tf_op jit(solution)/shard_map/ppermute | solution.py:21
  14.3 6.2 %collective-permute-start.2 = (bf16[5,3,1,256]{3,2,0,1:T(2,128)(2,1)S(1)}, bf16[5,3,1,256]{3,2,0,1:T(2,128)(2,1)S(1)}, u32[]{:S(2)}, u32[]{:S(2)}) collective-permute-start(bf16[5,3,1,256]{3,2,0,1:T(2,128)(2,1)S(1)} %get-tuple-element.84), channel_id=1, source_target_pairs={{0,1},{1,2},{2,3},{3,4},{4,5},{5,6},{6,7},{7,0},{8,9},{9,10},{10,1... | collective-permute-start | bytes 23048 | tf_op jit(solution)/shard_map/ppermute | solution.py:18
  21.7 5.7 %collective-permute-start.5 = (bf16[5,1,8,256]{3,2,0,1:T(8,128)(2,1)S(1)}, bf16[5,1,8,256]{3,2,0,1:T(8,128)(2,1)S(1)}, u32[]{:S(2)}, u32[]{:S(2)}) collective-permute-start(bf16[5,1,8,256]{3,2,0,1:T(8,128)(2,1)S(1)} %get-tuple-element.59), channel_id=1, source_target_pairs={{8,0},{16,8},{24,16},{32,24},{40,32},{48,40},{56,48},{64,56},{72,6... | collective-permute-start | bytes 61448 | tf_op jit(solution)/shard_map/ppermute | solution.py:21
  26.6 1.8 %collective-permute-start.4 = (bf16[5,1,8,256]{3,2,0,1:T(8,128)(2,1)S(1)}, bf16[5,1,8,256]{3,2,0,1:T(8,128)(2,1)S(1)}, u32[]{:S(2)}, u32[]{:S(2)}) collective-permute-start(bf16[5,1,8,256]{3,2,0,1:T(8,128)(2,1)S(1)} %get-tuple-element.59), channel_id=1, source_target_pairs={{0,8},{8,16},{16,24},{24,32},{32,40},{40,48},{48,56},{56,64},{64,7... | collective-permute-start | bytes 61448 | tf_op jit(solution)/shard_map/ppermute | solution.py:18
  28.4 4.2 %collective-permute-start.7 = (bf16[5,3,1,256]{3,2,0,1:T(2,128)(2,1)S(1)}, bf16[5,3,1,256]{3,2,0,1:T(2,128)(2,1)S(1)}, u32[]{:S(2)}, u32[]{:S(2)}) collective-permute-start(bf16[5,3,1,256]{3,2,0,1:T(2,128)(2,1)S(1)} %get-tuple-element.83), channel_id=1, source_target_pairs={{1,0},{2,1},{3,2},{4,3},{5,4},{6,5},{7,6},{0,7},{9,8},{10,9},{11,1... | collective-permute-start | bytes 23048 | tf_op jit(solution)/shard_map/ppermute | solution.py:21
  29.1 6.2 %collective-permute-start.6 = (bf16[5,3,1,256]{3,2,0,1:T(2,128)(2,1)S(1)}, bf16[5,3,1,256]{3,2,0,1:T(2,128)(2,1)S(1)}, u32[]{:S(2)}, u32[]{:S(2)}) collective-permute-start(bf16[5,3,1,256]{3,2,0,1:T(2,128)(2,1)S(1)} %get-tuple-element.82), channel_id=1, source_target_pairs={{0,1},{1,2},{2,3},{3,4},{4,5},{5,6},{6,7},{7,0},{8,9},{9,10},{10,1... | collective-permute-start | bytes 23048 | tf_op jit(solution)/shard_map/ppermute | solution.py:18
  35.8 7.0 %collective-permute-start.9 = (bf16[5,1,8,256]{3,2,0,1:T(8,128)(2,1)S(1)}, bf16[5,1,8,256]{3,2,0,1:T(8,128)(2,1)S(1)}, u32[]{:S(2)}, u32[]{:S(2)}) collective-permute-start(bf16[5,1,8,256]{3,2,0,1:T(8,128)(2,1)S(1)} %fusion.75), channel_id=1, source_target_pairs={{8,0},{16,8},{24,16},{32,24},{40,32},{48,40},{56,48},{64,56},{72,6... | collective-permute-start | bytes 61448 | tf_op jit(solution)/shard_map/ppermute | solution.py:21
  41.9 1.2 collective-permute-start.8
  43.2 4.2 %collective-permute-start.11 = (bf16[5,3,1,256]{3,2,0,1:T(2,128)(2,1)S(1)}, bf16[5,3,1,256]{3,2,0,1:T(2,128)(2,1)S(1)}, u32[]{:S(2)}, u32[]{:S(2)}) collective-permute-start(bf16[5,3,1,256]{3,2,0,1:T(2,128)(2,1)S(1)} %get-tuple-element.81), channel_id=1, source_target_pairs={{1,0},{2,1},{3,2},{4,3},{5,4},{6,5},{7,6},{0,7},{9,8},{10,9},{11,1... | collective-permute-start | bytes 23048 | tf_op jit(solution)/shard_map/ppermute | solution.py:21
  43.2 6.3 %collective-permute-start.10 = (bf16[5,3,1,256]{3,2,0,1:T(2,128)(2,1)S(1)}, bf16[5,3,1,256]{3,2,0,1:T(2,128)(2,1)S(1)}, u32[]{:S(2)}, u32[]{:S(2)}) collective-permute-start(bf16[5,3,1,256]{3,2,0,1:T(2,128)(2,1)S(1)} %get-tuple-element.80), channel_id=1, source_target_pairs={{0,1},{1,2},{2,3},{3,4},{4,5},{5,6},{6,7},{7,0},{8,9},{9,10},{10,1... | collective-permute-start | bytes 23048 | tf_op jit(solution)/shard_map/ppermute | solution.py:18
  49.7 19.1 %copy-start.1 = (bf16[124,5,1,2048]{3,0,2,1:T(8,128)(2,1)S(1)}, bf16[124,5,1,2048]{3,0,2,1:T(8,128)(2,1)}, u32[]{:S(2)}) copy-start(bf16[124,5,1,2048]{3,0,2,1:T(8,128)(2,1)} %param.3) | copy-start | bytes 7618564
  49.9 6.3 %collective-permute-start.13 = (bf16[5,1,8,256]{3,2,0,1:T(8,128)(2,1)S(1)}, bf16[5,1,8,256]{3,2,0,1:T(8,128)(2,1)S(1)}, u32[]{:S(2)}, u32[]{:S(2)}) collective-permute-start(bf16[5,1,8,256]{3,2,0,1:T(8,128)(2,1)S(1)} %get-tuple-element.25), channel_id=1, source_target_pairs={{8,0},{16,8},{24,16},{32,24},{40,32},{48,40},{56,48},{64,56},{72,6... | collective-permute-start | bytes 61448 | tf_op jit(solution)/shard_map/ppermute | solution.py:21
  55.4 1.2 collective-permute-start.12
  56.6 4.2 %collective-permute-start.15 = (bf16[5,3,1,256]{3,2,0,1:T(2,128)(2,1)S(1)}, bf16[5,3,1,256]{3,2,0,1:T(2,128)(2,1)S(1)}, u32[]{:S(2)}, u32[]{:S(2)}) collective-permute-start(bf16[5,3,1,256]{3,2,0,1:T(2,128)(2,1)S(1)} %get-tuple-element.79), channel_id=1, source_target_pairs={{1,0},{2,1},{3,2},{4,3},{5,4},{6,5},{7,6},{0,7},{9,8},{10,9},{11,1... | collective-permute-start | bytes 23048 | tf_op jit(solution)/shard_map/ppermute | solution.py:21
  56.7 6.3 %collective-permute-start.14 = (bf16[5,3,1,256]{3,2,0,1:T(2,128)(2,1)S(1)}, bf16[5,3,1,256]{3,2,0,1:T(2,128)(2,1)S(1)}, u32[]{:S(2)}, u32[]{:S(2)}) collective-permute-start(bf16[5,3,1,256]{3,2,0,1:T(2,128)(2,1)S(1)} %get-tuple-element.78), channel_id=1, source_target_pairs={{0,1},{1,2},{2,3},{3,4},{4,5},{5,6},{6,7},{7,0},{8,9},{9,10},{10,1... | collective-permute-start | bytes 23048 | tf_op jit(solution)/shard_map/ppermute | solution.py:18
  65.5 9.9 %all-to-all-start = ((bf16[8,2,2560]{2,1,0:T(2,128)(2,1)}), bf16[8,2,2560]{2,1,0:T(2,128)(2,1)S(1)}, u32[]{:S(2)}, u32[]{:S(2)}) async-start(bf16[8,2,2560]{2,1,0:T(2,128)(2,1)} %reshape.677), calls=%async_computation | async-start | bytes 163840 | tf_op jit(solution)/shard_map/all_to_all | solution.py:91
